TPU v7x, 32 devices: a whole 2x2x4 slice. The times are simulated.
32 devices in a mesh: tm: 4 (over x, core), vox: 8 (over z, y).
Axes of the slice: x: 2, y: 2, z: 4, core: 2. Of those that a mesh axis runs over, the one named last changes fastest.
Arguments:
- clip_features: bfloat16 [1024, 1024], P('tm'), may hold values from -6 to 6
- depth_kernel: float32 [3, 1024], replicated, may hold values from -3.5 to 3.5
- point_weight: bfloat16 [1024, 1024], replicated, may hold values from -0.1875 to 0.1875
- session_lengths: int32 [8], replicated, may hold values from 1 to 256, 1024 in all
- subject_feature_gains: float32 [16, 1024], replicated, may hold values from 0.25 to 1.75
- readout_weight: bfloat16 [1024, 5120], P(None, 'vox'), may hold values from -0.1875 to 0.1875
- hrf_kernel: float32 [16, 5120], P(None, 'vox'), may hold values from -1.5 to 1.5
- block_subject: int32 [40], P('vox'), may hold values from 0 to 15, as said below
- block_live: int32 [40], P('vox'), may hold values from 0 to 128, as said below
- bold_target: bfloat16 [1024, 5120], P('tm', 'vox'), may hold values from -6 to 6
Outputs:
- loss_total: float32 [], replicated
- grad_readout: float32 [1024, 5120], P('tm', 'vox')
- grad_point: float32 [1024, 1024], P(None, 'vox')
Inputs may be any that keep to these rules, and one draw needn't show every extreme that they name: `session_lengths`: the lengths sum to 1024; one session has exactly 256 TRs. `block_subject`: ids never fall along the blocks; every subject owns one or two consecutive blocks, subject 0 two; the blocks after the last subject's live ones carry id 16 - 1 and no live voxels. `block_live`: the live voxels of a block are its first slots; a subject's blocks are full except its last, which holds at least one live voxel; blocks after the subjects' blocks are empty.
All inputs are finite; a program needn't handle non-finite values.
Results may differ from a plain program's by a relative error of at most 0.0044.
Values may be sent and summed in bfloat16 or wider, within the bound.
No kernel may reach another device: no remote copies, remote signals or barrier semaphores. Data moves between devices by JAX's collectives and lax.ppermute only.
A program may use at most 64 MiB of HBM per device.

v0:
```python
import jax
import jax.numpy as jnp
from jax import lax
from jax.sharding import PartitionSpec as P

BLOCK_VOX = 128
KERNEL_TAPS = 3
TAP_SPACING = 8
HRF = 16


def from_behind(value, axis, steps):
    count = lax.axis_size(axis)
    first, last = (max(0, -steps), min(count, count - steps))
    return lax.ppermute(value, axis, [(source, source + steps) for source in range(first, last)])


def session_of(session_ends, position):
    return jnp.sum((session_ends[None, :] <= position[:, None]).astype(jnp.int32), axis=1)


def live_block(operands):
    return jnp.dot(operands[0], operands[1], preferred_element_type=jnp.float32).astype(
        jnp.bfloat16
    )


def dead_block(operands):
    return jnp.zeros((operands[0].shape[0], operands[1].shape[1]), jnp.bfloat16)


def shards(
    clip_features,
    depth_kernel,
    point_weight,
    session_lengths,
    subject_feature_gains,
    readout_weight,
    hrf_kernel,
    block_subject,
    block_live,
    bold_target,
):
    local_rows = clip_features.shape[0]
    feature_count = clip_features.shape[1]
    slot_count = readout_weight.shape[1]
    block_count = slot_count // BLOCK_VOX
    subjects = subject_feature_gains.shape[0]
    total_rows = local_rows * lax.axis_size("tm")
    first_row = lax.axis_index("tm") * local_rows
    core_margin_rows = (KERNEL_TAPS - 1) * TAP_SPACING
    filter_rim = HRF - 1
    session_ends = jnp.cumsum(session_lengths)
    earlier = from_behind(clip_features[local_rows - core_margin_rows :], "tm", 1)
    extended = jnp.concatenate([earlier, clip_features], axis=0)
    ext_position = (
        first_row - core_margin_rows + jnp.arange(core_margin_rows + local_rows, dtype=jnp.int32)
    )
    ext_session = session_of(session_ends, ext_position)
    out_rows = core_margin_rows + local_rows - core_margin_rows
    out_session = ext_session[core_margin_rows:]
    depth_sum = jnp.zeros((out_rows, feature_count), jnp.float32)
    for kernel_tap_index in range(KERNEL_TAPS):
        shift_amount = core_margin_rows - kernel_tap_index * TAP_SPACING
        source = extended[shift_amount : shift_amount + out_rows].astype(jnp.float32)
        valid_tap = (ext_position[shift_amount : shift_amount + out_rows] >= 0) & (
            ext_session[shift_amount : shift_amount + out_rows] == out_session
        )
        depth_sum = depth_sum + depth_kernel[kernel_tap_index][None, :] * jnp.where(
            valid_tap[:, None], source, 0.0
        )
    depth_half = depth_sum.astype(jnp.bfloat16)
    pre_act = jnp.dot(depth_half, point_weight, preferred_element_type=jnp.float32)
    core_out = (extended[core_margin_rows:].astype(jnp.float32) + jax.nn.gelu(pre_act)).astype(
        jnp.bfloat16
    )
    one_hot = (block_subject[:, None] == jnp.arange(subjects, dtype=jnp.int32)[None, :]).astype(
        jnp.float32
    )
    gain_rows = jnp.dot(one_hot, subject_feature_gains, precision=lax.Precision.HIGHEST)
    scale_cols = jnp.transpose(gain_rows)[:, :, None]
    effective = (
        (
            readout_weight.astype(jnp.float32).reshape(feature_count, block_count, BLOCK_VOX)
            * scale_cols
        )
        .reshape(feature_count, slot_count)
        .astype(jnp.bfloat16)
    )
    pieces = []
    for block_index in range(block_count):
        weight_cols = effective[:, block_index * BLOCK_VOX : (block_index + 1) * BLOCK_VOX]
        pieces.append(
            lax.cond(block_live[block_index] > 0, live_block, dead_block, (core_out, weight_cols))
        )
    response = jnp.concatenate(pieces, axis=1)
    response_before = from_behind(response[local_rows - filter_rim :], "tm", 1)
    response_ext = jnp.concatenate([response_before, response], axis=0)
    filter_position = first_row - filter_rim + jnp.arange(filter_rim + local_rows, dtype=jnp.int32)
    filter_session = session_of(session_ends, filter_position)
    own_session = filter_session[filter_rim:]
    predicted = jnp.zeros((local_rows, slot_count), jnp.float32)
    for kernel_tap_index in range(HRF):
        shift_amount = filter_rim - kernel_tap_index
        source = response_ext[shift_amount : shift_amount + local_rows].astype(jnp.float32)
        valid_tap = (filter_position[shift_amount : shift_amount + local_rows] >= 0) & (
            filter_session[shift_amount : shift_amount + local_rows] == own_session
        )
        predicted = predicted + hrf_kernel[kernel_tap_index][None, :] * jnp.where(
            valid_tap[:, None], source, 0.0
        )
    local_counts = jnp.dot(block_live.astype(jnp.float32), one_hot, precision=lax.Precision.HIGHEST)
    subject_voxels = lax.psum(local_counts, "vox")
    block_voxels = jnp.dot(one_hot, subject_voxels, precision=lax.Precision.HIGHEST)
    live_mask = (
        (jnp.arange(BLOCK_VOX, dtype=jnp.int32)[None, :] < block_live[:, None])
        .astype(jnp.float32)
        .reshape(slot_count)
    )
    voxel_weight = live_mask / jnp.repeat(block_voxels, BLOCK_VOX)
    misfit = predicted - bold_target.astype(jnp.float32)
    partial_loss = jnp.sum(voxel_weight[None, :] * misfit * misfit)
    loss_total = lax.psum(partial_loss, ("tm", "vox")) / (subjects * total_rows)
    pred_grad = 2.0 * voxel_weight[None, :] * misfit
    later = from_behind(pred_grad[:filter_rim], "tm", -1)
    grad_ext = jnp.concatenate([pred_grad, later], axis=0)
    later_position = first_row + jnp.arange(local_rows + filter_rim, dtype=jnp.int32)
    later_session = session_of(session_ends, later_position)
    response_grad = jnp.zeros((local_rows, slot_count), jnp.float32)
    for kernel_tap_index in range(HRF):
        source = grad_ext[kernel_tap_index : kernel_tap_index + local_rows]
        valid_tap = (
            later_position[kernel_tap_index : kernel_tap_index + local_rows] < total_rows
        ) & (later_session[kernel_tap_index : kernel_tap_index + local_rows] == own_session)
        response_grad = response_grad + hrf_kernel[kernel_tap_index][None, :] * jnp.where(
            valid_tap[:, None], source, 0.0
        )
    response_half = response_grad.astype(jnp.bfloat16)
    raw_rows = lax.dot_general(
        core_out, response_half, (((0,), (0,)), ((), ())), preferred_element_type=jnp.float32
    )
    grad_readout = lax.psum_scatter(
        (
            raw_rows.reshape(
                lax.axis_size("tm") * (feature_count // lax.axis_size("tm")), block_count, BLOCK_VOX
            )
            * jnp.transpose(gain_rows)[:, :, None]
        ).reshape(lax.axis_size("tm") * (feature_count // lax.axis_size("tm")), slot_count),
        "tm",
        scatter_dimension=0,
        tiled=True,
    )
    share_width = feature_count // lax.axis_size("vox")
    col_start = lax.axis_index("vox") * share_width
    pre_cols = lax.dynamic_slice_in_dim(pre_act, col_start, share_width, 1)
    full_grad = lax.dot_general(
        response_half, effective, (((1,), (1,)), ((), ())), preferred_element_type=jnp.float32
    )
    summed_grad = lax.psum(full_grad, "vox")
    grad_cols = lax.dynamic_slice_in_dim(summed_grad, col_start, share_width, 1)
    pre_grad = jax.vjp(jax.nn.gelu, pre_cols)[1](grad_cols)[0].astype(jnp.bfloat16)
    point_part = lax.dot_general(
        depth_half, pre_grad, (((0,), (0,)), ((), ())), preferred_element_type=jnp.float32
    )
    grad_point = lax.psum(point_part, "tm")
    return (loss_total, grad_readout, grad_point)


def solution(mesh):
    placed = (
        P("tm", None),
        P(),
        P(),
        P(),
        P(),
        P(None, "vox"),
        P(None, "vox"),
        P("vox"),
        P("vox"),
        P("tm", "vox"),
    )
    return jax.shard_map(
        shards,
        mesh=mesh,
        in_specs=placed,
        out_specs=(P(), P("tm", "vox"), P(None, "vox")),
        check_vma=False,
    )
```

profile of v0, /device:TPU:0, one launch (start us, length us, event | category | flops | bytes accessed | tf_op | source)
XLA Modules:
  0.0 259.4 jit_solution(6205240970641587257)
XLA Ops:
  8.1 2.3 collective-permute-start
  15.5 22.5 %psum.28 = f32[16]{0:T(128)S(1)} all-reduce(f32[16]{0:T(128)S(1)} %convolution_bitcast_fusion.2), channel_id=1, replica_groups=mesh['tm'=4,'vox'=8] {'vox'}, use_global_device_ids=true, to_apply=%region_0.0 | all-reduce | flops 16 | bytes 128 | tf_op jit(solution)/shard_map/psum | solution.py:113
  47.1 2.5 copy.21
  49.7 1.7 multiply_convert_fusion
  52.0 2.0 fusion.9
  54.0 2.8 %conditional.5 = (bf16[256,128]{1,0:T(8,128)(2,1)S(1)}) conditional(s32[]{:T(128)} %bitcast.5, () %tuple.38, (bf16[1024,640]{0,1:T(8,128)(2,1)S(1)}, bf16[256,1024]{1,0:T(8,128)(2,1)}) %tuple.45), branch_computations={%region_3.4_spmd, %region_4.5_spmd} | conditional | flops 67141632 | bytes 3473416 | solution.py:94
  57.5 2.8 %conditional.9 = (bf16[256,128]{1,0:T(8,128)(2,1)S(1)}) conditional(s32[]{:T(128)} %bitcast.16, () %tuple.43, (bf16[1024,640]{0,1:T(8,128)(2,1)S(1)}, bf16[256,1024]{1,0:T(8,128)(2,1)}) %tuple.45), branch_computations={%region_11.12_spmd, %region_12.13_spmd} | conditional | flops 67141632 | bytes 3473416 | solution.py:94
  60.4 3.5 %conditional.8 = (bf16[256,128]{1,0:T(8,128)(2,1)}) conditional(s32[]{:T(128)} %bitcast.15, () %tuple.42, (bf16[1024,640]{0,1:T(8,128)(2,1)S(1)}, bf16[256,1024]{1,0:T(8,128)(2,1)}) %tuple.45), branch_computations={%region_9.10_spmd, %region_10.11_spmd} | conditional | flops 67141632 | bytes 3473416 | solution.py:94
  61.9 2.0 convolution_convert_fusion.3
  63.9 3.5 %conditional.7 = (bf16[256,128]{1,0:T(8,128)(2,1)}) conditional(s32[]{:T(128)} %bitcast.14, () %tuple.41, (bf16[1024,640]{0,1:T(8,128)(2,1)S(1)}, bf16[256,1024]{1,0:T(8,128)(2,1)}) %tuple.45), branch_computations={%region_7.8_spmd, %region_8.9_spmd} | conditional | flops 67141632 | bytes 3473416 | solution.py:94
  65.3 2.0 convolution_convert_fusion.2
  67.4 3.5 %conditional.6 = (bf16[256,128]{1,0:T(8,128)(2,1)}) conditional(s32[]{:T(128)} %bitcast.13, () %tuple.40, (bf16[1024,640]{0,1:T(8,128)(2,1)S(1)}, bf16[256,1024]{1,0:T(8,128)(2,1)}) %tuple.45), branch_computations={%region_5.6_spmd, %region_6.7_spmd} | conditional | flops 67141632 | bytes 3473416 | solution.py:94
  68.8 2.0 convolution_convert_fusion.1
  79.3 9.5 %broadcast_multiply_fusion = (f32[256,640]{1,0:T(8,128)S(1)}, f32[256,640]{1,0:T(8,128)}) fusion(f32[640]{0:T(1024)S(1)} %broadcast_multiply_fusion.1, bf16[256,640]{1,0:T(8,128)(2,1)} %param.29, bf16[256,640]{1,0:T(8,128)(2,1)} %constant_dynamic-update-slice_fusion.2, bf16[15,640]{1,0:T(8,128)(2,1)S(1)} %collective-permute-done.1, ...), kind=kLoop, calls=%fused_computation.154 | loop fusion | flops 18186240 | bytes 2032896 | tf_op jit(solution)/shard_map/mul | solution.py:124
  90.3 3.6 %collective-permute-done.2 = f32[15,640]{1,0:T(8,128)S(1)} collective-permute-done((f32[15,640]{1,0:T(8,128)S(1)}, f32[15,640]{1,0:T(8,128)S(1)}, u32[]{:S(2)}, u32[]{:S(2)}) %collective-permute-start.2) | collective-permute-done | bytes 38432 | tf_op jit(solution)/shard_map/ppermute | solution.py:15
  94.0 3.4 %fusion.23 = bf16[256,640]{1,0:T(8,128)(2,1)S(1)} fusion(f32[15,640]{1,0:T(8,128)S(1)} %collective-permute-done.2, f32[256,640]{1,0:T(8,128)S(1)} %get-tuple-element.91, f32[640]{0:T(1024)S(1)} %get-tuple-element.87, f32[640]{0:T(1024)S(1)} %get-tuple-element.88, f32[640]{0:T(1024)S(1)} %get-tuple-element.74, f32[640]{0:T(1024)S(1)} %get-tuple-element.75, ...), kind=kLoop, calls=%fused_computation.65 | loop fusion | flops 10321920 | bytes 1066496 | tf_op jit(solution)/shard_map/convert_element_type | solution.py:138
  99.8 1.9 mul.406
  101.7 3.3 %copy.27 = f32[1024,640]{1,0:T(8,128)} copy(f32[1024,640]{0,1:T(8,128)} %bitcast.41) | data formatting | bytes 5242880 | tf_op jit(solution)/shard_map/mul | solution.py:84
  104.9 71.6 %all-reduce.3.cloned.1.call-done = f32[256,1024]{1,0:T(8,128)} async-done(((f32[256,1024]{1,0:T(8,128)}), f32[256,1024]{1,0:T(8,128)}) %all-reduce.3.cloned.1.call-update) | async-done | bytes 1048592 | tf_op jit(solution)/shard_map/psum | solution.py:159
  176.5 2.1 fusion.99
  178.8 4.0 %convolution_multiply_fusion = f32[1024,640]{1,0:T(8,128)} fusion(f32[1024,640]{1,0:T(8,128)} %copy.27, bf16[256,1024]{1,0:T(8,128)(2,1)} %get-tuple-element.136, bf16[256,640]{1,0:T(8,128)(2,1)S(1)} %copy-done.2), kind=kOutput, calls=%fused_computation.39 | convolution fusion | flops 336199680 | bytes 6094848 | tf_op jit(solution)/shard_map/dot_general | solution.py:139
  184.7 39.8 %psum.29 = f32[]{:T(128)} all-reduce(f32[]{:T(128)} %fusion.17), channel_id=1, replica_groups=mesh['tm'=4,'vox'=8] {'tm','vox'}, use_global_device_ids=true, to_apply=%region_15.16 | all-reduce | flops 1 | bytes 8 | tf_op jit(solution)/shard_map/psum | solution.py:123
  225.2 24.7 %reduce-scatter.2.cloned.1.call-done = f32[256,640]{1,0:T(8,128)} async-done(((f32[1024,640]{1,0:T(8,128)}), f32[256,640]{1,0:T(8,128)}) %reduce-scatter.2.cloned.1.call-update) | async-done | bytes 655376 | tf_op jit(solution)/shard_map/reduce_scatter | solution.py:142
  249.9 1.9 copy.45
  (91 shorter events, 37.2 us)
Async XLA Ops:
  7.2 44.8 %copy-start = (bf16[1024,1024]{1,0:T(8,128)(2,1)S(1)}, bf16[1024,1024]{1,0:T(8,128)(2,1)}, u32[]{:S(2)}) copy-start(bf16[1024,1024]{1,0:T(8,128)(2,1)} %param.22) | copy-start | bytes 6291460
  7.2 169.4 %all-reduce.3.cloned.1.call-start = ((), (), s32[]{:S(2)}) async-start(), calls=%async_computation.2 | async-start | bytes 2097152 | tf_op jit(solution)/shard_map/psum | solution.py:159
  8.1 43.2 %collective-permute-start = (bf16[16,1024]{1,0:T(8,128)(2,1)S(1)}, bf16[16,1024]{1,0:T(8,128)(2,1)S(1)}, u32[]{:S(2)}, u32[]{:S(2)}) collective-permute-start(bf16[16,1024]{1,0:T(8,128)(2,1)S(1)} %slice.434), channel_id=1, source_target_pairs={{0,8},{8,16},{16,24},{1,9},{9,17},{17,25},{2,10},{10,18},{18,26},{... | collective-permute-start | bytes 98312 | tf_op jit(solution)/shard_map/ppermute | solution.py:15
  38.9 0.8 copy-start.18
  49.6 1.7 copy-start.4
  49.6 1.8 copy-start.15
  49.6 1.8 copy-start.16
  49.7 1.8 copy-start.17
  52.0 2.1 copy-start.5
  73.8 20.1 %copy-start.8 = (pred[256]{0:T(512)(128)(4,1)S(1)}, pred[256]{0:T(512)(128)(4,1)}, u32[]{:S(2)}) copy-start(pred[256]{0:T(512)(128)(4,1)} %get-tuple-element.107) | copy-start | bytes 772
  73.8 20.1 %copy-start.9 = (pred[256]{0:T(512)(128)(4,1)S(1)}, pred[256]{0:T(512)(128)(4,1)}, u32[]{:S(2)}) copy-start(pred[256]{0:T(512)(128)(4,1)} %get-tuple-element.96) | copy-start | bytes 772
  73.8 20.1 %copy-start.10 = (pred[256]{0:T(512)(128)(4,1)S(1)}, pred[256]{0:T(512)(128)(4,1)}, u32[]{:S(2)}) copy-start(pred[256]{0:T(512)(128)(4,1)} %get-tuple-element.97) | copy-start | bytes 772
  73.8 20.1 %copy-start.11 = (pred[256]{0:T(512)(128)(4,1)S(1)}, pred[256]{0:T(512)(128)(4,1)}, u32[]{:S(2)}) copy-start(pred[256]{0:T(512)(128)(4,1)} %get-tuple-element.98) | copy-start | bytes 772
  73.8 20.1 %copy-start.12 = (pred[256]{0:T(512)(128)(4,1)S(1)}, pred[256]{0:T(512)(128)(4,1)}, u32[]{:S(2)}) copy-start(pred[256]{0:T(512)(128)(4,1)} %get-tuple-element.99) | copy-start | bytes 772
  73.8 20.1 %copy-start.13 = (pred[256]{0:T(512)(128)(4,1)S(1)}, pred[256]{0:T(512)(128)(4,1)}, u32[]{:S(2)}) copy-start(pred[256]{0:T(512)(128)(4,1)} %get-tuple-element.100) | copy-start | bytes 772
  73.8 20.1 %copy-start.14 = (pred[256]{0:T(512)(128)(4,1)S(1)}, pred[256]{0:T(512)(128)(4,1)}, u32[]{:S(2)}) copy-start(pred[256]{0:T(512)(128)(4,1)} %get-tuple-element.101) | copy-start | bytes 772
  76.7 2.6 %collective-permute-start.1 = (bf16[15,640]{1,0:T(8,128)(2,1)S(1)}, bf16[15,640]{1,0:T(8,128)(2,1)S(1)}, u32[]{:S(2)}, u32[]{:S(2)}) collective-permute-start(bf16[15,640]{1,0:T(8,128)(2,1)S(1)} %slice.561), channel_id=1, source_target_pairs={{0,8},{8,16},{16,24},{1,9},{9,17},{17,25},{2,10},{10,18},{18,26},{... | collective-permute-start | bytes 57608 | tf_op jit(solution)/shard_map/ppermute | solution.py:15
  88.9 5.0 %collective-permute-start.2 = (f32[15,640]{1,0:T(8,128)S(1)}, f32[15,640]{1,0:T(8,128)S(1)}, u32[]{:S(2)}, u32[]{:S(2)}) collective-permute-start(f32[15,640]{1,0:T(8,128)S(1)} %slice.590), channel_id=1, source_target_pairs={{8,0},{16,8},{24,16},{9,1},{17,9},{25,17},{10,2},{18,10},{26,18},{... | collective-permute-start | bytes 115208 | tf_op jit(solution)/shard_map/ppermute | solution.py:15
  97.4 0.8 copy-start.1
  99.7 125.5 %all-reduce.5.cloned.1.call-start = ((), (), s32[]{:S(2)}) async-start(), calls=%async_computation.3 | async-start | bytes 1048576 | tf_op jit(solution)/shard_map/psum | solution.py:165
  101.7 74.9 %copy-start.6 = (bf16[256,1024]{1,0:T(8,128)(2,1)S(1)}, bf16[256,1024]{1,0:T(8,128)(2,1)}, u32[]{:S(2)}) copy-start(bf16[256,1024]{1,0:T(8,128)(2,1)} %copy-done.5) | copy-start | bytes 1572868
  104.9 73.8 %copy-start.2 = (bf16[256,640]{1,0:T(8,128)(2,1)S(1)}, bf16[256,640]{1,0:T(8,128)(2,1)}, u32[]{:S(2)}) copy-start(bf16[256,640]{1,0:T(8,128)(2,1)} %copy-done.1) | copy-start | bytes 983044
  178.7 71.2 %reduce-scatter.2.cloned.1.call-start = ((), (), s32[]{:S(2)}) async-start(), calls=%async_computation.1 | async-start | bytes 3276800 | tf_op jit(solution)/shard_map/reduce_scatter | solution.py:142
  182.8 1.1 copy-start.3
  (2 other events, 1.3 us)
Sparse Core Ops, SparseCore 0:
  99.9 76.6 all-reduce.2
  179.0 32.8 all-reduce.4
  215.2 34.6 reduce-scatter.1
where the time goes:
time: 261 us; the launch traced here: 259 us
  waiting for transfers between devices  100 us (38%)
  blocking collectives  62.3 us (24%)
  local copies, waits for them, and re-layouts  29.8 us (11%)
  other arithmetic  21.8 us (8%)
  matrix products  21.4 us (8%)
  between operations  19.2 us (7%)
  starting transfers between devices  5.04 us (2%)
    psum x1, waiting for transfers between devices, shards(): summed_grad = lax.psum(full_grad, 'vox')  71.6 us
    psum x1, blocking collectives, shards(): loss_total = lax.psum(partial_loss, ('tm', 'vox')) / (subjects * total_rows)  39.8 us
    reduce_scatter x1, waiting for transfers between devices, shards(): lax.psum_scatter((raw_rows.reshape(lax.axis_size('tm') * (feature_count /...  24.7 us
    psum x1, blocking collectives, shards(): subject_voxels = lax.psum(local_counts, 'vox')  22.5 us
    unnamed x47, local copies, waits for them, and re-layouts  11.3 us
    mul x2, other arithmetic, shards(): pred_grad = 2.0 * voxel_weight[None, :] * misfit  10.3 us
    dot_general x5, matrix products, live_block(): jnp.dot(operands[0], operands[1], preferred_element_type=jnp.float32)  8.82 us
    another operation x5, local copies, waits for them, and re-layouts  7.27 us
  transfers between devices with their start and end apart: 6, of which 3 were waited for; matrix products, arithmetic and copies ran while one was open for 10% of the time, Pallas kernels for 0%

commit v1 on v0

--- a/solution.py
+++ b/solution.py
@@ -156,7 +156,7 @@
     full_grad = lax.dot_general(
         response_half, effective, (((1,), (1,)), ((), ())), preferred_element_type=jnp.float32
     )
-    summed_grad = lax.psum(full_grad, "vox")
+    summed_grad = jnp.sum(lax.all_gather(full_grad, "vox"), axis=0)
     grad_cols = lax.dynamic_slice_in_dim(summed_grad, col_start, share_width, 1)
     pre_grad = jax.vjp(jax.nn.gelu, pre_cols)[1](grad_cols)[0].astype(jnp.bfloat16)
     point_part = lax.dot_general(

time: 261 us -> 279 us (1.069)
  waiting for transfers between devices: 100 us -> 118 us
  other arithmetic: 21.8 us -> 27.5 us
  local copies, waits for them, and re-layouts: 29.8 us -> 26.2 us
    all_gather x0 -> x1, waiting for transfers between devices: none -> 114 us  [shards(): summed_grad = jnp.sum(lax.all_gather(full_grad, 'vox'), axis=0)]
    psum x1 -> x0, waiting for transfers between devices: 71.6 us -> none  [shards(): summed_grad = lax.psum(full_grad, 'vox')]
    reduce_scatter x1, waiting for transfers between devices: 24.7 us -> 0.03 us  [shards(): lax.psum_scatter((raw_rows.reshape(lax.axis_size('tm') * (feature_count /...]
    reduce_sum x0 -> x1, other arithmetic: none -> 5.49 us  [shards(): summed_grad = jnp.sum(lax.all_gather(full_grad, 'vox'), axis=0)]
    unnamed x47 -> x49, local copies, waits for them, and re-layouts: 11.3 us -> 7.74 us
  transfers between devices with their start and end apart: 6 -> 6, of which waited for: 3 -> 2; matrix products, arithmetic and copies ran while one was open for 10% -> 12% of each run, Pallas kernels for 0% -> 0%
where the time goes in v1:
time: 279 us; the launch traced here: 278 us
  waiting for transfers between devices  118 us (42%)
  blocking collectives  61.1 us (22%)
  other arithmetic  27.5 us (10%)
  local copies, waits for them, and re-layouts  26.2 us (9%)
  between operations  20.8 us (7%)
  matrix products  19.8 us (7%)
  starting transfers between devices  5.04 us (2%)
    all_gather x1, waiting for transfers between devices, shards(): summed_grad = jnp.sum(lax.all_gather(full_grad, 'vox'), axis=0)  114 us
    psum x1, blocking collectives, shards(): loss_total = lax.psum(partial_loss, ('tm', 'vox')) / (subjects * total_rows)  38.6 us
    psum x1, blocking collectives, shards(): subject_voxels = lax.psum(local_counts, 'vox')  22.5 us
    mul x2, other arithmetic, shards(): pred_grad = 2.0 * voxel_weight[None, :] * misfit  10.4 us
    unnamed x49, local copies, waits for them, and re-layouts  7.74 us
    another operation x5, local copies, waits for them, and re-layouts  7.26 us
    dot_general x5, matrix products, live_block(): jnp.dot(operands[0], operands[1], preferred_element_type=jnp.float32)  6.96 us
  transfers between devices with their start and end apart: 6, of which 2 were waited for; matrix products, arithmetic and copies ran while one was open for 12% of the time, Pallas kernels for 0%

profile of v1, /device:TPU:0, one launch (start us, length us, event | category | flops | bytes accessed | tf_op | source)
XLA Modules:
  0.0 278.2 jit_solution(8788514093957331023)
XLA Ops:
  9.0 2.3 collective-permute-start
  16.5 22.5 %psum.21 = f32[16]{0:T(128)S(1)} all-reduce(f32[16]{0:T(128)S(1)} %convolution_bitcast_fusion.2), channel_id=1, replica_groups=mesh['tm'=4,'vox'=8] {'vox'}, use_global_device_ids=true, to_apply=%region_0.0 | all-reduce | flops 16 | bytes 128 | tf_op jit(solution)/shard_map/psum | solution.py:113
  45.3 2.5 copy.21
  50.4 1.7 multiply_convert_fusion
  52.7 2.0 fusion.9
  54.8 2.8 %conditional.5 = (bf16[256,128]{1,0:T(8,128)(2,1)S(1)}) conditional(s32[]{:T(128)} %bitcast.5, () %tuple.38, (bf16[1024,640]{0,1:T(8,128)(2,1)S(1)}, bf16[256,1024]{1,0:T(8,128)(2,1)}) %tuple.45), branch_computations={%region_3.4_spmd, %region_4.5_spmd} | conditional | flops 67141632 | bytes 3473416 | solution.py:94
  54.8 1.5 copy.22
  58.2 2.8 %conditional.6 = (bf16[256,128]{1,0:T(8,128)(2,1)S(1)}) conditional(s32[]{:T(128)} %bitcast.13, () %tuple.40, (bf16[1024,640]{0,1:T(8,128)(2,1)S(1)}, bf16[256,1024]{1,0:T(8,128)(2,1)}) %tuple.45), branch_computations={%region_5.6_spmd, %region_6.7_spmd} | conditional | flops 67141632 | bytes 3473416 | solution.py:94
  58.3 1.5 copy.23
  61.7 2.8 %conditional.7 = (bf16[256,128]{1,0:T(8,128)(2,1)S(1)}) conditional(s32[]{:T(128)} %bitcast.14, () %tuple.41, (bf16[1024,640]{0,1:T(8,128)(2,1)S(1)}, bf16[256,1024]{1,0:T(8,128)(2,1)}) %tuple.45), branch_computations={%region_7.8_spmd, %region_8.9_spmd} | conditional | flops 67141632 | bytes 3473416 | solution.py:94
  65.2 2.8 %conditional.8 = (bf16[256,128]{1,0:T(8,128)(2,1)S(1)}) conditional(s32[]{:T(128)} %bitcast.15, () %tuple.42, (bf16[1024,640]{0,1:T(8,128)(2,1)S(1)}, bf16[256,1024]{1,0:T(8,128)(2,1)}) %tuple.45), branch_computations={%region_9.10_spmd, %region_10.11_spmd} | conditional | flops 67141632 | bytes 3473416 | solution.py:94
  68.7 2.8 %conditional.9 = (bf16[256,128]{1,0:T(8,128)(2,1)S(1)}) conditional(s32[]{:T(128)} %bitcast.16, () %tuple.43, (bf16[1024,640]{0,1:T(8,128)(2,1)S(1)}, bf16[256,1024]{1,0:T(8,128)(2,1)}) %tuple.45), branch_computations={%region_11.12_spmd, %region_12.13_spmd} | conditional | flops 67141632 | bytes 3473416 | solution.py:94
  75.7 9.7 %broadcast_multiply_fusion = (f32[256,640]{1,0:T(8,128)S(1)}, f32[256,640]{1,0:T(8,128)}) fusion(f32[640]{0:T(1024)S(1)} %broadcast_multiply_fusion.1, bf16[256,640]{1,0:T(8,128)(2,1)} %param.29, bf16[256,640]{1,0:T(8,128)(2,1)} %constant_dynamic-update-slice_fusion.2, bf16[15,640]{1,0:T(8,128)(2,1)S(1)} %collective-permute-done.1, ...), kind=kLoop, calls=%fused_computation.154 | loop fusion | flops 18186240 | bytes 2032896 | tf_op jit(solution)/shard_map/mul | solution.py:124
  86.7 3.6 %collective-permute-done.2 = f32[15,640]{1,0:T(8,128)S(1)} collective-permute-done((f32[15,640]{1,0:T(8,128)S(1)}, f32[15,640]{1,0:T(8,128)S(1)}, u32[]{:S(2)}, u32[]{:S(2)}) %collective-permute-start.2) | collective-permute-done | bytes 38432 | tf_op jit(solution)/shard_map/ppermute | solution.py:15
  90.4 3.4 %fusion.23 = bf16[256,640]{1,0:T(8,128)(2,1)S(1)} fusion(f32[15,640]{1,0:T(8,128)S(1)} %collective-permute-done.2, f32[256,640]{1,0:T(8,128)S(1)} %get-tuple-element.91, f32[640]{0:T(1024)S(1)} %get-tuple-element.87, f32[640]{0:T(1024)S(1)} %get-tuple-element.88, f32[640]{0:T(1024)S(1)} %get-tuple-element.74, f32[640]{0:T(1024)S(1)} %get-tuple-element.75, ...), kind=kLoop, calls=%fused_computation.65 | loop fusion | flops 10321920 | bytes 1066496 | tf_op jit(solution)/shard_map/convert_element_type | solution.py:138
  94.6 1.6 fusion.120
  96.2 1.9 mul.406
  98.1 3.4 %copy.27 = f32[1024,640]{1,0:T(8,128)} copy(f32[1024,640]{0,1:T(8,128)} %bitcast.42) | data formatting | bytes 5242880 | tf_op jit(solution)/shard_map/mul | solution.py:84
  101.5 4.3 %convolution_multiply_fusion = f32[1024,640]{1,0:T(8,128)} fusion(f32[1024,640]{1,0:T(8,128)} %copy.27, bf16[256,1024]{1,0:T(8,128)(2,1)S(1)} %copy-done.7, bf16[256,640]{1,0:T(8,128)(2,1)S(1)} %copy-done.2), kind=kOutput, calls=%fused_computation.39 | convolution fusion | flops 336199680 | bytes 6094848 | tf_op jit(solution)/shard_map/dot_general | solution.py:139
  105.9 113.9 %all-gather.3.cloned.1.call-done = f32[2048,1024]{1,0:T(8,128)} async-done(((f32[256,1024]{1,0:T(8,128)}), f32[2048,1024]{1,0:T(8,128)}) %all-gather.3.cloned.1.call-update) | async-done | bytes 8388624 | tf_op jit(solution)/shard_map/all_gather | solution.py:159
  219.8 5.5 %reduce_sum.49 = f32[256,1024]{1,0:T(8,128)} reduce(f32[8,256,1024]{2,1,0:T(8,128)} %bitcast.43, f32[]{:T(128)} %constant.25.clone.1), dimensions={0}, to_apply=%region_18.19 | reduce | flops 1835008 | bytes 9437188 | tf_op jit(solution)/shard_map/reduce_sum | solution.py:159
  225.3 2.2 fusion.99
  228.4 38.6 %psum.22 = f32[]{:T(128)} all-reduce(f32[]{:T(128)} %fusion.17), channel_id=1, replica_groups=mesh['tm'=4,'vox'=8] {'tm','vox'}, use_global_device_ids=true, to_apply=%region_15.16 | all-reduce | flops 1 | bytes 8 | tf_op jit(solution)/shard_map/psum | solution.py:123
  267.8 1.9 copy.44
  (94 shorter events, 33.4 us)
Async XLA Ops:
  8.0 44.7 %copy-start = (bf16[1024,1024]{1,0:T(8,128)(2,1)S(1)}, bf16[1024,1024]{1,0:T(8,128)(2,1)}, u32[]{:S(2)}) copy-start(bf16[1024,1024]{1,0:T(8,128)(2,1)} %param.22) | copy-start | bytes 6291460
  8.0 211.8 %all-gather.3.cloned.1.call-start = ((), (), s32[]{:S(2)}) async-start(), calls=%async_computation.3 | async-start | bytes 9437184 | tf_op jit(solution)/shard_map/all_gather | solution.py:159
  9.0 43.1 %collective-permute-start = (bf16[16,1024]{1,0:T(8,128)(2,1)S(1)}, bf16[16,1024]{1,0:T(8,128)(2,1)S(1)}, u32[]{:S(2)}, u32[]{:S(2)}) collective-permute-start(bf16[16,1024]{1,0:T(8,128)(2,1)S(1)} %slice.434), channel_id=1, source_target_pairs={{0,8},{8,16},{16,24},{1,9},{9,17},{17,25},{2,10},{10,18},{18,26},{... | collective-permute-start | bytes 98312 | tf_op jit(solution)/shard_map/ppermute | solution.py:15
  50.4 1.8 copy-start.16
  50.4 1.8 copy-start.17
  50.4 1.8 copy-start.18
  52.7 2.1 copy-start.5
  71.6 18.8 %copy-start.9 = (pred[256]{0:T(512)(128)(4,1)S(1)}, pred[256]{0:T(512)(128)(4,1)}, u32[]{:S(2)}) copy-start(pred[256]{0:T(512)(128)(4,1)} %get-tuple-element.101) | copy-start | bytes 772
  71.6 18.8 %copy-start.10 = (pred[256]{0:T(512)(128)(4,1)S(1)}, pred[256]{0:T(512)(128)(4,1)}, u32[]{:S(2)}) copy-start(pred[256]{0:T(512)(128)(4,1)} %get-tuple-element.102) | copy-start | bytes 772
  71.6 18.8 %copy-start.11 = (pred[256]{0:T(512)(128)(4,1)S(1)}, pred[256]{0:T(512)(128)(4,1)}, u32[]{:S(2)}) copy-start(pred[256]{0:T(512)(128)(4,1)} %get-tuple-element.103) | copy-start | bytes 772
  71.6 18.8 %copy-start.12 = (pred[256]{0:T(512)(128)(4,1)S(1)}, pred[256]{0:T(512)(128)(4,1)}, u32[]{:S(2)}) copy-start(pred[256]{0:T(512)(128)(4,1)} %get-tuple-element.104) | copy-start | bytes 772
  71.6 18.8 %copy-start.13 = (pred[256]{0:T(512)(128)(4,1)S(1)}, pred[256]{0:T(512)(128)(4,1)}, u32[]{:S(2)}) copy-start(pred[256]{0:T(512)(128)(4,1)} %get-tuple-element.105) | copy-start | bytes 772
  71.6 18.8 %copy-start.14 = (pred[256]{0:T(512)(128)(4,1)S(1)}, pred[256]{0:T(512)(128)(4,1)}, u32[]{:S(2)}) copy-start(pred[256]{0:T(512)(128)(4,1)} %get-tuple-element.106) | copy-start | bytes 772
  71.6 18.8 %copy-start.15 = (pred[256]{0:T(512)(128)(4,1)S(1)}, pred[256]{0:T(512)(128)(4,1)}, u32[]{:S(2)}) copy-start(pred[256]{0:T(512)(128)(4,1)} %get-tuple-element.107) | copy-start | bytes 772
  73.0 2.6 collective-permute-start.1
  85.4 5.0 %collective-permute-start.2 = (f32[15,640]{1,0:T(8,128)S(1)}, f32[15,640]{1,0:T(8,128)S(1)}, u32[]{:S(2)}, u32[]{:S(2)}) collective-permute-start(f32[15,640]{1,0:T(8,128)S(1)} %slice.590), channel_id=1, source_target_pairs={{8,0},{16,8},{24,16},{9,1},{17,9},{25,17},{10,2},{18,10},{26,18},{... | collective-permute-start | bytes 115208 | tf_op jit(solution)/shard_map/ppermute | solution.py:15
  96.2 171.5 %reduce-scatter.2.cloned.1.call-start = ((), (), s32[]{:S(2)}) async-start(), calls=%async_computation.1 | async-start | bytes 3276800 | tf_op jit(solution)/shard_map/reduce_scatter | solution.py:142
  98.1 3.4 %copy-start.2 = (bf16[256,640]{1,0:T(8,128)(2,1)S(1)}, bf16[256,640]{1,0:T(8,128)(2,1)}, u32[]{:S(2)}) copy-start(bf16[256,640]{1,0:T(8,128)(2,1)} %copy-done.1) | copy-start | bytes 983044
  98.1 3.4 %copy-start.7 = (bf16[256,1024]{1,0:T(8,128)(2,1)S(1)}, bf16[256,1024]{1,0:T(8,128)(2,1)}, u32[]{:S(2)}) copy-start(bf16[256,1024]{1,0:T(8,128)(2,1)} %get-tuple-element.136) | copy-start | bytes 1572868
  105.9 161.9 %all-reduce.2.cloned.1.call-start = ((), (), s32[]{:S(2)}) async-start(), calls=%async_computation.2 | async-start | bytes 1048576 | tf_op jit(solution)/shard_map/psum | solution.py:165
  219.8 5.5 %copy-start.6 = (bf16[256,1024]{1,0:T(8,128)(2,1)S(1)}, bf16[256,1024]{1,0:T(8,128)(2,1)}, u32[]{:S(2)}) copy-start(bf16[256,1024]{1,0:T(8,128)(2,1)} %copy-done.5) | copy-start | bytes 1572868
  225.3 2.3 copy-start.8
  225.3 2.3 copy-start.20
  225.3 2.4 copy-start.3
  (3 other events, 3.2 us)
Sparse Core Ops, SparseCore 0:
  96.3 123.4 all-gather.2
Sparse Core Ops, SparseCore 1:
  105.9 33.1 reduce-scatter.1
  227.6 31.4 all-reduce.1
